TPU v7x, 32 devices: a whole 2x2x4 slice. The times are simulated.
32 devices in a mesh: segment: 4 (over z), ctx: 4 (over y, x), tp: 2 (over core).
Axes of the slice: x: 2, y: 2, z: 4, core: 2. Of those that a mesh axis runs over, the one named last changes fastest.
Arguments:
- queries: bfloat16 [4, 512, 8, 640], P('segment', 'ctx', 'tp'), may hold values from -200 to 200
- pairs: bfloat16 [4, 512, 8, 256], P('segment', 'ctx', 'tp'), may hold values from -6 to 6
- out_proj: bfloat16 [4, 8, 640, 5120], P('segment', 'tp'), may hold values from -0.625 to 0.625
- lengths: int32 [4, 4], replicated, may hold values from 1 to 256, 512 in all within a row
Outputs:
- scored: bfloat16 [4, 512, 5120], P('segment', 'ctx', 'tp')
Inputs may be any that keep to these rules, and one draw needn't show every extreme that they name: `lengths`: each row sums to 512; its largest length is exactly 256.
All inputs are finite; a program needn't handle non-finite values.
Results may differ from a plain program's by a relative error of at most 0.014.
Values may be sent and summed in bfloat16 or wider, within the bound.
A program may use at most 64 MiB of HBM per device.

v0:
```python
import functools
import math

import jax
import jax.numpy as jnp
from jax import lax
from jax.experimental import pallas as pl
from jax.experimental.pallas import tpu as pltpu
from jax.sharding import PartitionSpec as P

MESH = pl.DeviceIdType.MESH
HIDDEN = -1e30


def tile_of(columns):
    for tile in (1280, 640, 512, 256, 128):
        if columns % tile == 0:
            return tile
    return columns


def kernel(
    sizes,
    lengths_hbm,
    q_ref,
    kv_ref,
    w_hbm,
    out_ref,
    lengths_ref,
    w_ref,
    seen_ref,
    hide_ref,
    sent_ref,
    got_ref,
    acc_ref,
    part_ref,
    share_ref,
    lengths_sem,
    w_sem,
    seen_send,
    seen_recv,
    att_send,
    att_recv,
    share_send,
    share_recv,
):
    n_seg, n_ctx, n_tp, rows, heads, head_dim, group, back = sizes
    seg = lax.axis_index("segment")
    ctx = lax.axis_index("ctx")
    tp = lax.axis_index("tp")
    width = group * head_dim
    columns = out_ref.shape[1]
    tile = tile_of(columns)
    tiles = columns // tile
    depth = (back + 1) * rows

    lengths_copy = pltpu.make_async_copy(lengths_hbm, lengths_ref, lengths_sem)
    lengths_copy.start()

    def w_copy(h):
        part = pl.ds(pl.multiple_of(h * width, width), width)
        return pltpu.make_async_copy(w_hbm.at[part], w_ref.at[part], w_sem.at[h])

    for h in range(heads):
        w_copy(h).start()

    barrier = pltpu.get_barrier_semaphore()
    greeted = jnp.int32(0)
    for by in range(1, back + 1):
        for peer in (ctx - by, ctx + by):
            valid = (peer >= 0) & (peer < n_ctx)
            greeted = greeted + valid.astype(jnp.int32)

            @pl.when(valid)
            def _():
                pl.semaphore_signal(
                    barrier, inc=1, device_id={"ctx": peer}, device_id_type=MESH
                )

    to_seg = lax.rem(seg + n_seg - 1, n_seg)
    from_seg = lax.rem(seg + 1, n_seg)
    for peer in (to_seg, from_seg):
        pl.semaphore_signal(
            barrier, inc=1, device_id={"segment": peer}, device_id_type=MESH
        )
    for by in range(1, n_tp):
        pl.semaphore_signal(
            barrier,
            inc=1,
            device_id={"tp": lax.rem(tp + by, n_tp)},
            device_id_type=MESH,
        )
    pl.semaphore_wait(barrier, greeted + 2 + n_tp - 1)

    def kv_send(by, h):
        part = pl.ds(pl.multiple_of(h * 2 * head_dim, 2 * head_dim), 2 * head_dim)
        return pltpu.make_async_remote_copy(
            src_ref=kv_ref.at[:, part],
            dst_ref=seen_ref.at[by - 1, :, part],
            send_sem=seen_send.at[by - 1, h],
            recv_sem=seen_recv.at[by - 1, h],
            device_id={"ctx": lax.rem(ctx + by, n_ctx)},
            device_id_type=MESH,
        )

    relayed = [h for h in range(heads) if h % 2 == 1] if n_ctx == 4 and back == 2 else []

    def direct(by, h):
        sends = ctx + by < n_ctx
        return sends & (ctx != 1) if by == 1 and h in relayed else sends

    def relay(h):
        part = pl.ds(pl.multiple_of(h * 2 * head_dim, 2 * head_dim), 2 * head_dim)
        return pltpu.make_async_remote_copy(
            src_ref=seen_ref.at[1, :, part],
            dst_ref=seen_ref.at[0, :, part],
            send_sem=seen_send.at[0, h],
            recv_sem=seen_recv.at[0, h],
            device_id={"ctx": 2},
            device_id_type=MESH,
        )

    for h in range(heads):
        for by in range(1, back + 1):

            @pl.when(direct(by, h))
            def _():
                kv_send(by, h).start()

    for by in range(1, back + 1):

        @pl.when(ctx < by)
        def _():
            seen_ref[by - 1] = jnp.zeros(seen_ref.shape[1:], seen_ref.dtype)

    lengths_copy.wait()
    query_pos = ctx * rows + lax.broadcasted_iota(jnp.int32, (rows, depth), 0)
    key_pos = (ctx - back) * rows + lax.broadcasted_iota(jnp.int32, (rows, depth), 1)
    first = jnp.zeros((rows, depth), jnp.int32)
    end = jnp.int32(0)
    for k in range(lengths_ref.shape[1]):
        end = end + lengths_ref[seg, k]
        first = jnp.where(query_pos >= end, end, first)
    visible = (key_pos >= first) & (key_pos <= query_pos)
    hide_ref[...] = jnp.where(visible, 0.0, HIDDEN)
    acc_ref[...] = jnp.zeros_like(acc_ref)

    factor = math.log2(math.e) / math.sqrt(head_dim)

    def att_copy(unit):
        return pltpu.make_async_remote_copy(
            src_ref=sent_ref.at[unit],
            dst_ref=got_ref.at[unit],
            send_sem=att_send.at[unit],
            recv_sem=att_recv.at[unit],
            device_id={"segment": to_seg},
            device_id_type=MESH,
        )

    def waits_here(h):
        here = jnp.bool_(True)
        for other in relayed:
            here = here & (h != other)
        return here

    def pass_on(h):
        @pl.when(ctx == 3)
        def _():
            kv_send(2, h).wait_recv()
            relay(h).start()

    def attend(h, carry):
        for by in range(back, 0, -1):

            known = ctx >= by
            if relayed and by == 2:
                known = known & ((ctx != 3) | waits_here(h))

            @pl.when(known)
            def _():
                kv_send(by, h).wait_recv()


        key_part = pl.ds(pl.multiple_of(h * 2 * head_dim, head_dim), head_dim)
        value_part = pl.ds(
            pl.multiple_of(h * 2 * head_dim + head_dim, head_dim), head_dim
        )
        blocks = [seen_ref.at[by - 1] for by in range(back, 0, -1)] + [kv_ref]
        keys = jnp.concatenate([block[:, key_part] for block in blocks], axis=0)
        values = jnp.concatenate([block[:, value_part] for block in blocks], axis=0)
        for g in range(group):
            at = pl.ds(pl.multiple_of((h * group + g) * head_dim, head_dim), head_dim)
            scores = lax.dot_general(
                q_ref[:, at],
                keys,
                (((1,), (1,)), ((), ())),
                preferred_element_type=jnp.float32,
            )
            scores = scores + hide_ref[...]
            peak = jnp.max(scores, axis=1, keepdims=True)
            weights = jnp.exp2((scores - peak) * factor)
            denom = jnp.sum(weights, axis=1, keepdims=True)
            mixed = jnp.dot(
                weights.astype(jnp.bfloat16), values, preferred_element_type=jnp.float32
            )
            sent_ref[h * group + g] = (mixed * (1.0 / denom)).astype(jnp.bfloat16)
            att_copy(h * group + g).start()
        return carry

    late = max(1, min(group - 1, 2))

    def total_of(h, begin, low, high, tile=tile):
        mixed = jnp.concatenate(
            [got_ref[h * group + g] for g in range(low, high)], axis=1
        )
        weight = w_ref[
            pl.ds(
                pl.multiple_of(h * width + low * head_dim, head_dim),
                (high - low) * head_dim,
            ),
            pl.ds(pl.multiple_of(begin, tile), tile),
        ]
        return acc_ref[:, pl.ds(pl.multiple_of(begin, tile), tile)] + jnp.dot(
            mixed, weight, preferred_element_type=jnp.float32
        )

    def project(h, low, high):
        for g in range(low, high):
            att_copy(h * group + g).wait_recv()

        def one(n, inner):
            begin = pl.multiple_of(n * columns, columns)
            acc_ref[:, pl.ds(begin, columns)] = total_of(h, begin, low, high, columns)
            return inner

        lax.fori_loop(0, n_tp, one, 0)

    def attend_and_project(h, carry):
        attend(h, 0)
        w_copy(h - 1).wait()
        project(h - 1, 0, group)
        return carry

    last = heads - 1
    for h in relayed:
        if h == 0:
            pass_on(h)
    attend(0, 0)
    for h in relayed:
        if h > 0:
            pass_on(h)
    lax.fori_loop(1, heads, attend_and_project, 0)
    w_copy(last).wait()
    project(last, 0, group - late)
    for g in range(group - late, group):
        att_copy(last * group + g).wait_recv()

    def share_copy(by, n):
        at = pl.ds(pl.multiple_of(n * tile, tile), tile)
        return pltpu.make_async_remote_copy(
            src_ref=part_ref.at[by - 1, :, at],
            dst_ref=share_ref.at[by - 1, :, at],
            send_sem=share_send.at[by - 1, n],
            recv_sem=share_recv.at[by - 1, n],
            device_id={"tp": lax.rem(tp + by, n_tp)},
            device_id_type=MESH,
        )

    for by in range(1, n_tp):
        peer = lax.rem(tp + by, n_tp)

        for n in range(tiles):
            at = pl.ds(pl.multiple_of(n * tile, tile), tile)
            part_ref[by - 1, :, at] = total_of(
                last, peer * columns + n * tile, group - late, group
            ).astype(jnp.bfloat16)
            share_copy(by, n).start()

    for n in range(tiles):
        total = total_of(last, tp * columns + n * tile, group - late, group)
        at = pl.ds(pl.multiple_of(n * tile, tile), tile)
        for by in range(1, n_tp):
            share_copy(by, n).wait_recv()
            total = total + share_ref[by - 1, :, at].astype(jnp.float32)
        out_ref[:, at] = total.astype(jnp.bfloat16)

    for unit in range(heads * group):
        att_copy(unit).wait_send()
    for h in range(heads):
        for by in range(1, back + 1):

            @pl.when(direct(by, h))
            def _():
                kv_send(by, h).wait_send()

        if h in relayed:

            @pl.when(ctx == 3)
            def _():
                relay(h).wait_send()

    for by in range(1, n_tp):
        for n in range(tiles):
            share_copy(by, n).wait_send()


def local(n_seg, n_ctx, n_tp, queries, pairs, out_proj, lengths):
    rows, heads = pairs.shape[1], pairs.shape[2]
    head_dim = pairs.shape[3] // 2
    width = queries.shape[3]
    group = width // head_dim
    model = out_proj.shape[3]
    columns = model // n_tp
    back = min(n_ctx - 1, -(-(rows * n_ctx // 2 - 1) // rows))
    tiles = columns // tile_of(columns)
    sizes = (n_seg, n_ctx, n_tp, rows, heads, head_dim, group, back)
    bf16 = jnp.bfloat16
    dma = pltpu.SemaphoreType.DMA
    result = pl.pallas_call(
        functools.partial(kernel, sizes),
        out_shape=jax.ShapeDtypeStruct((rows, columns), bf16),
        in_specs=[
            pl.BlockSpec(memory_space=pltpu.HBM),
            pl.BlockSpec(memory_space=pltpu.VMEM),
            pl.BlockSpec(memory_space=pltpu.VMEM),
            pl.BlockSpec(memory_space=pl.ANY),
        ],
        out_specs=pl.BlockSpec(memory_space=pltpu.VMEM),
        scratch_shapes=[
            pltpu.SMEM(lengths.shape, jnp.int32),
            pltpu.VMEM((heads * width, model), bf16),
            pltpu.VMEM((back, rows, heads * 2 * head_dim), bf16),
            pltpu.VMEM((rows, (back + 1) * rows), jnp.float32),
            pltpu.VMEM((heads * group, rows, head_dim), bf16),
            pltpu.VMEM((heads * group, rows, head_dim), bf16),
            pltpu.VMEM((rows, model), jnp.float32),
            pltpu.VMEM((n_tp - 1, rows, columns), bf16),
            pltpu.VMEM((n_tp - 1, rows, columns), bf16),
            dma,
            dma((heads,)),
            dma((back, heads)),
            dma((back, heads)),
            dma((heads * group,)),
            dma((heads * group,)),
            dma((n_tp - 1, tiles)),
            dma((n_tp - 1, tiles)),
        ],
        compiler_params=pltpu.CompilerParams(
            collective_id=0, has_side_effects=True, vmem_limit_bytes=40 << 20
        ),
    )(
        lengths,
        queries.reshape(rows, heads * width),
        pairs.reshape(rows, heads * 2 * head_dim),
        out_proj.reshape(heads * width, model),
    )
    return result.reshape(1, rows, columns)


def solution(mesh):
    sizes = [mesh.shape[axis] for axis in ("segment", "ctx", "tp")]
    return jax.shard_map(
        functools.partial(local, *sizes),
        mesh=mesh,
        in_specs=(
            P("segment", "ctx", "tp", None),
            P("segment", "ctx", "tp", None),
            P("segment", "tp", None, None),
            P(),
        ),
        out_specs=P("segment", "ctx", "tp"),
        check_vma=False,
    )
```

profile of v0, /device:TPU:21, one launch (start us, length us, event | category | flops | bytes accessed | tf_op | source)
XLA Modules:
  0.0 32.8 jit_solution(16409916640720999523)
XLA Ops:
  0.0 1.0 %copy.6 = bf16[16,8,4,256]{3,1,2,0:T(8,128)(2,1)S(1)} copy(bf16[16,8,4,256]{3,2,1,0:T(4,128)(2,1)} %bitcast.13) | data formatting | bytes 524288
  1.0 1.2 %copy.5 = bf16[16,8,4,640]{3,1,2,0:T(8,128)(2,1)S(1)} copy(bf16[16,8,4,640]{3,2,1,0:T(4,128)(2,1)} %bitcast.12) | data formatting | bytes 1310720
  2.2 0.0 copy-start
  2.2 0.7 %copy-done = s32[4,4]{1,0:T(4,128)S(1)} copy-done((s32[4,4]{1,0:T(4,128)S(1)}, s32[4,4]{1,0:T(4,128)}, u32[]{:S(2)}) %copy-start) | copy-done | bytes 88
  2.8 29.1 %shard_map.46 = bf16[128,2560]{1,0:T(8,128)(2,1)S(1)} custom-call(s32[4,4]{1,0:T(4,128)S(1)} %copy-done, bf16[128,2560]{1,0:T(8,128)(2,1)S(1)} %bitcast.9, bf16[128,1024]{1,0:T(8,128)(2,1)S(1)} %bitcast.10, bf16[2560,5120]{1,0:T(8,128)(2,1)} %bitcast.11), custom_call_target="tpu_custom_call" | custom-call | tf_op jit(solution)/shard_map/pallas_call | solution.py:319
  32.0 0.8 %copy.8 = bf16[1,128,2560]{2,1,0:T(8,128)(2,1)} copy(bf16[1,128,2560]{2,1,0:T(8,128)(2,1)S(1)} %bitcast.8) | data formatting | bytes 1310720
Async XLA Ops:
  2.2 0.7 %copy-start = (s32[4,4]{1,0:T(4,128)S(1)}, s32[4,4]{1,0:T(4,128)}, u32[]{:S(2)}) copy-start(s32[4,4]{1,0:T(4,128)} %lengths_hbm.1) | copy-start | bytes 196
where the time goes:
time: 33 us; the launch traced here: 32.8 us
  Pallas kernels  29.1 us (88%)
  local copies, waits for them, and re-layouts  3.66 us (11%)
    pallas_call x1, Pallas kernels, local(): pl.pallas_call(functools.partial(kernel, sizes), out_shape=jax.ShapeDtype...  29.1 us
    unnamed x5, local copies, waits for them, and re-layouts  3.66 us

commit v1 on v0

v1 whole, which is shorter than its diff:
```python
import functools
import math

import jax
import jax.numpy as jnp
from jax import lax
from jax.experimental import pallas as pl
from jax.experimental.layout import Layout, with_layout_constraint
from jax.experimental.pallas import tpu as pltpu
from jax.sharding import PartitionSpec as P

MESH = pl.DeviceIdType.MESH
HIDDEN = -1e30


def tile_of(columns):
    for tile in (1280, 640, 512, 256, 128):
        if columns % tile == 0:
            return tile
    return columns


def kernel(
    sizes,
    lengths_hbm,
    q_hbm,
    kv_hbm,
    w_hbm,
    out_ref,
    lengths_ref,
    q_raw,
    kv_raw,
    q_wide,
    kv_wide,
    q_ref,
    kv_ref,
    ship_q,
    ship_kv,
    w_ref,
    last_w,
    seen_ref,
    hide_ref,
    sent_ref,
    got_ref,
    peer_got,
    acc_ref,
    part_ref,
    share_ref,
    lengths_sem,
    raw_sem,
    w_sem,
    own_w_sem,
    peer_w_send,
    peer_w_recv,
    ship_send,
    ship_recv,
    seen_send,
    seen_recv,
    att_send,
    att_recv,
    fwd_send,
    fwd_recv,
    share_send,
    share_recv,
):
    n_seg, n_ctx, n_tp, rows, heads, head_dim, group, back, shipped = sizes
    seg = lax.axis_index("segment")
    ctx = lax.axis_index("ctx")
    tp = lax.axis_index("tp")
    width = group * head_dim
    columns = out_ref.shape[1]
    tile = tile_of(columns)
    tiles = columns // tile
    depth = (back + 1) * rows
    own = heads - shipped
    last = own - 1
    early = [h for h in range(heads) if h != last]
    to_seg = lax.rem(seg + n_seg - 1, n_seg)
    from_seg = lax.rem(seg + 1, n_seg)
    relays = n_ctx == 4 and back == 2

    def relayed(h):
        return relays and h > 0

    lengths_copy = pltpu.make_async_copy(lengths_hbm, lengths_ref, lengths_sem)
    kv_copy = pltpu.make_async_copy(kv_hbm, kv_raw, raw_sem.at[0])
    q_copy = pltpu.make_async_copy(q_hbm, q_raw, raw_sem.at[1])
    kv_copy.start()
    q_copy.start()
    lengths_copy.start()

    barrier = pltpu.get_barrier_semaphore()

    def sends_to(source, by, h=0):
        there = (source >= 0) & (source + by < n_ctx)
        return there & (source != 1) if relayed(h) and by == 1 else there

    awaited = jnp.int32(1 + n_tp - 1)
    pl.semaphore_signal(
        barrier, inc=1, device_id={"segment": from_seg}, device_id_type=MESH
    )
    for by in range(1, back + 1):
        awaited = awaited + sends_to(ctx, by).astype(jnp.int32)

        @pl.when(sends_to(ctx - by, by))
        def _():
            pl.semaphore_signal(
                barrier, inc=1, device_id={"ctx": ctx - by}, device_id_type=MESH
            )

    if relays:
        awaited = awaited + (ctx == 3).astype(jnp.int32)

        @pl.when(ctx == 2)
        def _():
            pl.semaphore_signal(
                barrier, inc=1, device_id={"ctx": 3}, device_id_type=MESH
            )

    for by in range(1, n_tp):
        pl.semaphore_signal(
            barrier,
            inc=1,
            device_id={"tp": lax.rem(tp + by, n_tp)},
            device_id_type=MESH,
        )

    def w_copy(n):
        return pltpu.make_async_copy(
            w_hbm.at[pl.ds(early[n] * width, width)],
            w_ref.at[pl.ds(n * width, width)],
            w_sem.at[n],
        )

    def own_w_copy(g):
        return pltpu.make_async_copy(
            w_hbm.at[
                pl.ds(last * width + g * head_dim, head_dim),
                pl.ds(pl.multiple_of(tp * columns, columns), columns),
            ],
            last_w.at[g, pl.ds(0, head_dim)],
            own_w_sem.at[g],
        )

    def peer_w_copy(by, g):
        peer = lax.rem(tp + by, n_tp)
        return pltpu.make_async_remote_copy(
            src_ref=w_hbm.at[
                pl.ds(last * width + g * head_dim, head_dim),
                pl.ds(pl.multiple_of(peer * columns, columns), columns),
            ],
            dst_ref=last_w.at[g, pl.ds(by * head_dim, head_dim)],
            send_sem=peer_w_send.at[by - 1, g],
            recv_sem=peer_w_recv.at[by - 1, g],
            device_id={"tp": peer},
            device_id_type=MESH,
        )

    def split_kv(h, ref):
        for part in range(2):
            ref[:, part * head_dim : (part + 1) * head_dim] = kv_wide[
                pl.ds(part * heads + h, rows, stride=2 * heads), :
            ].astype(jnp.bfloat16)

    def split_q(h, ref, base):
        for g in range(group):
            ref[base + g] = q_wide[
                pl.ds(g * heads + h, rows, stride=group * heads), :
            ].astype(jnp.bfloat16)

    kv_copy.wait()
    kv_wide[...] = kv_raw[...].astype(jnp.float32)
    for h in range(own):
        split_kv(h, kv_ref.at[h])
    if shipped:
        split_kv(own, ship_kv)
    q_copy.wait()
    q_wide[...] = q_raw[...].astype(jnp.float32)
    if shipped:
        split_q(own, ship_q, 0)

    pl.semaphore_wait(barrier, awaited)

    def ship(n):
        return pltpu.make_async_remote_copy(
            src_ref=(ship_kv, ship_q)[n],
            dst_ref=(kv_ref.at[own], q_ref.at[pl.ds(own * group, group)])[n],
            send_sem=ship_send.at[n],
            recv_sem=ship_recv.at[n],
            device_id={"segment": to_seg},
            device_id_type=MESH,
        )

    def kv_send(by, h):
        return pltpu.make_async_remote_copy(
            src_ref=kv_ref.at[h],
            dst_ref=seen_ref.at[h, by - 1],
            send_sem=seen_send.at[by - 1, h],
            recv_sem=seen_recv.at[by - 1, h],
            device_id={"ctx": lax.rem(ctx + by, n_ctx)},
            device_id_type=MESH,
        )

    def relay(h):
        return pltpu.make_async_remote_copy(
            src_ref=seen_ref.at[h, 1],
            dst_ref=seen_ref.at[h, 0],
            send_sem=seen_send.at[0, h],
            recv_sem=seen_recv.at[0, h],
            device_id={"ctx": 2},
            device_id_type=MESH,
        )

    def spread(h):
        for by in range(back, 0, -1):

            @pl.when(sends_to(ctx, by, h))
            def _():
                kv_send(by, h).start()

    if shipped:
        for n in range(2):
            ship(n).start()
    for h in range(own):
        spread(h)
    for n in range(len(early)):
        w_copy(n).start()
    for g in range(group):
        own_w_copy(g).start()
        for by in range(1, n_tp):
            peer_w_copy(by, g).start()

    for by in range(1, back + 1):

        @pl.when(ctx < by)
        def _():
            for h in range(heads):
                seen_ref[h, by - 1] = jnp.zeros((rows, 2 * head_dim), seen_ref.dtype)

    for h in range(own):
        split_q(h, q_ref, h * group)

    lengths_copy.wait()
    query_pos = ctx * rows + lax.broadcasted_iota(jnp.int32, (rows, depth), 0)
    key_pos = (ctx - back) * rows + lax.broadcasted_iota(jnp.int32, (rows, depth), 1)

    def hide(n, batch):
        first = jnp.zeros((rows, depth), jnp.int32)
        end = jnp.int32(0)
        for k in range(lengths_ref.shape[1]):
            end = end + lengths_ref[batch, k]
            first = jnp.where(query_pos >= end, end, first)
        visible = (key_pos >= first) & (key_pos <= query_pos)
        hide_ref[n] = jnp.where(visible, 0.0, HIDDEN)

    hide(0, seg)
    if shipped:
        hide(1, from_seg)

    factor = math.log2(math.e) / math.sqrt(head_dim)

    def att_copy(unit):
        return pltpu.make_async_remote_copy(
            src_ref=sent_ref.at[unit],
            dst_ref=got_ref.at[unit],
            send_sem=att_send.at[unit],
            recv_sem=att_recv.at[unit],
            device_id={"segment": to_seg},
            device_id_type=MESH,
        )

    def receive(h):
        if relayed(h):

            @pl.when(ctx == 3)
            def _():
                kv_send(2, h).wait_recv()
                relay(h).start()

        for by in range(back, 0, -1):
            known = ctx >= by
            if relayed(h) and by == 2:
                known = ctx == 2

            @pl.when(known)
            def _():
                kv_send(by, h).wait_recv()

    def attend(h, hidden, ref):
        blocks = [seen_ref.at[h, by - 1] for by in range(back, 0, -1)] + [kv_ref.at[h]]
        keys = jnp.concatenate([block[:, :head_dim] for block in blocks], axis=0)
        values = jnp.concatenate([block[:, head_dim:] for block in blocks], axis=0)
        for low in range(0, group, CHUNK):
            high = min(group, low + CHUNK)
            many = high - low
            queries = q_ref[h * group + low : h * group + high].reshape(
                many * rows, head_dim
            )
            scores = lax.dot_general(
                queries,
                keys,
                (((1,), (1,)), ((), ())),
                preferred_element_type=jnp.float32,
            )
            scores = (
                scores.reshape(many, rows, depth) + hide_ref[hidden][None]
            ).reshape(many * rows, depth)
            peak = jnp.max(scores, axis=1, keepdims=True)
            weights = jnp.exp2((scores - peak) * factor)
            denom = jnp.sum(weights, axis=1, keepdims=True)
            mixed = jnp.dot(
                weights.astype(jnp.bfloat16), values, preferred_element_type=jnp.float32
            )
            ref[h * group + low : h * group + high] = (
                (mixed * (1.0 / denom)).astype(jnp.bfloat16).reshape(many, rows, head_dim)
            )

    def arrived(h):
        if h < own:
            for g in range(group):
                att_copy(h * group + g).wait_recv()

    def total_of(n, begin, size):
        at = pl.ds(pl.multiple_of(begin, size), size)
        h = early[n]
        mixed = jnp.concatenate([got_ref[h * group + g] for g in range(group)], axis=1)
        product = jnp.dot(
            mixed,
            w_ref[pl.ds(n * width, width), at],
            preferred_element_type=jnp.float32,
        )
        return product if h == order[0] else acc_ref[:, at] + product

    def project(h):
        n = early.index(h)

        def one(k, carry):
            begin = pl.multiple_of(k * columns, columns)
            acc_ref[:, pl.ds(begin, columns)] = total_of(n, begin, columns)
            return carry

        lax.fori_loop(0, n_tp, one, 0)

    for h in range(own):
        receive(h)
        attend(h, 0, sent_ref)
        for g in range(group):
            att_copy(h * group + g).start()
        if shipped and h == 0:
            ship(0).wait_recv()
            spread(own)
    if shipped:
        receive(own)
        ship(1).wait_recv()
        attend(own, 1, got_ref)

    order = [h for h in early if h >= own] + [h for h in early if h < own]

    def share_copy(by, n):
        at = pl.ds(n * tile, tile)
        return pltpu.make_async_remote_copy(
            src_ref=part_ref.at[by - 1, :, at],
            dst_ref=share_ref.at[by - 1, :, at],
            send_sem=share_send.at[by - 1, n],
            recv_sem=share_recv.at[by - 1, n],
            device_id={"tp": lax.rem(tp + by, n_tp)},
            device_id_type=MESH,
        )

    def forward(by, g):
        return pltpu.make_async_remote_copy(
            src_ref=got_ref.at[last * group + g],
            dst_ref=peer_got.at[by - 1, g],
            send_sem=fwd_send.at[by - 1, g],
            recv_sem=fwd_recv.at[by - 1, g],
            device_id={"tp": lax.rem(tp + by, n_tp)},
            device_id_type=MESH,
        )

    def hand_on(g):
        att_copy(last * group + g).wait_recv()
        for by in range(1, n_tp):
            forward(by, g).start()

    handed = 0
    for h in order:
        arrived(h)
        w_copy(early.index(h)).wait()
        if h != order[-1]:
            project(h)
            continue
        for by in range(1, n_tp):
            peer = lax.rem(tp + by, n_tp)
            for n in range(tiles):
                part_ref[by - 1, :, pl.ds(n * tile, tile)] = total_of(
                    early.index(h), peer * columns + n * tile, tile
                ).astype(jnp.bfloat16)
                share_copy(by, n).start()
        handed = handed + 1
        hand_on(0)
        begin = pl.multiple_of(tp * columns, columns)
        acc_ref[:, pl.ds(begin, columns)] = total_of(
            early.index(h), begin, columns
        )

    def finish(g):
        own_w_copy(g).wait()
        for by in range(1, n_tp):
            peer_w_copy(by, g).wait_recv()
            forward(by, g).wait_recv()
        mixed = jnp.concatenate(
            [got_ref[last * group + g]] + [peer_got[by - 1, g] for by in range(1, n_tp)],
            axis=1,
        )
        into = pl.ds(pl.multiple_of(tp * columns, columns), columns)
        total = jnp.dot(mixed, last_w[g], preferred_element_type=jnp.float32)
        if order or g > 0:
            total = total + acc_ref[:, into]
        if g < group - 1:
            acc_ref[:, into] = total
            return
        if order:
            for by in range(1, n_tp):
                for n in range(tiles):
                    share_copy(by, n).wait_recv()
                total = total + share_ref[by - 1].astype(jnp.float32)
        out_ref[...] = total.astype(jnp.bfloat16)

    for g in range(group):
        if g >= handed:
            hand_on(g)
        if g > 0:
            finish(g - 1)
    finish(group - 1)

    for unit in range(own * group):
        att_copy(unit).wait_send()
    for h in range(heads):
        for by in range(1, back + 1):

            @pl.when(sends_to(ctx, by, h))
            def _():
                kv_send(by, h).wait_send()

        if relayed(h):

            @pl.when(ctx == 3)
            def _():
                relay(h).wait_send()

    if shipped:
        for n in range(2):
            ship(n).wait_send()
    for by in range(1, n_tp):
        for g in range(group):
            peer_w_copy(by, g).wait_send()
            forward(by, g).wait_send()
        if order:
            for n in range(tiles):
                share_copy(by, n).wait_send()


CHUNK = 5


def local(n_seg, n_ctx, n_tp, queries, pairs, out_proj, lengths):
    rows, heads = pairs.shape[1], pairs.shape[2]
    head_dim = pairs.shape[3] // 2
    width = queries.shape[3]
    group = width // head_dim
    model = out_proj.shape[3]
    columns = model // n_tp
    back = min(n_ctx - 1, -(-(rows * n_ctx // 2 - 1) // rows))
    tiles = columns // tile_of(columns)
    shipped = 1 if heads > 1 else 0
    own = heads - shipped
    sizes = (n_seg, n_ctx, n_tp, rows, heads, head_dim, group, back, shipped)
    bf16, f32 = jnp.bfloat16, jnp.float32
    dma = pltpu.SemaphoreType.DMA
    anywhere = pl.BlockSpec(memory_space=pl.ANY)

    def flat(array, parts):
        array = with_layout_constraint(
            array.reshape(rows, heads, parts, head_dim),
            Layout(major_to_minor=(0, 2, 1, 3)),
        )
        return array.transpose(0, 2, 1, 3).reshape(rows * parts * heads, head_dim)

    result = pl.pallas_call(
        functools.partial(kernel, sizes),
        out_shape=jax.ShapeDtypeStruct((rows, columns), bf16),
        in_specs=[anywhere] * 4,
        out_specs=pl.BlockSpec(memory_space=pltpu.VMEM),
        scratch_shapes=[
            pltpu.SMEM(lengths.shape, jnp.int32),
            pltpu.VMEM((rows * group * heads, head_dim), bf16),
            pltpu.VMEM((rows * 2 * heads, head_dim), bf16),
            pltpu.VMEM((rows * group * heads, head_dim), f32),
            pltpu.VMEM((rows * 2 * heads, head_dim), f32),
            pltpu.VMEM((heads * group, rows, head_dim), bf16),
            pltpu.VMEM((heads, rows, 2 * head_dim), bf16),
            pltpu.VMEM((group, rows, head_dim), bf16),
            pltpu.VMEM((rows, 2 * head_dim), bf16),
            pltpu.VMEM((max(1, heads - 1) * width, model), bf16),
            pltpu.VMEM((group, n_tp * head_dim, columns), bf16),
            pltpu.VMEM((heads, back, rows, 2 * head_dim), bf16),
            pltpu.VMEM((1 + shipped, rows, (back + 1) * rows), f32),
            pltpu.VMEM((own * group, rows, head_dim), bf16),
            pltpu.VMEM((heads * group, rows, head_dim), bf16),
            pltpu.VMEM((n_tp - 1, group, rows, head_dim), bf16),
            pltpu.VMEM((rows, model), f32),
            pltpu.VMEM((n_tp - 1, rows, columns), bf16),
            pltpu.VMEM((n_tp - 1, rows, columns), bf16),
            dma,
            dma((2,)),
            dma((max(1, heads - 1),)),
            dma((group,)),
            dma((n_tp - 1, group)),
            dma((n_tp - 1, group)),
            dma((2,)),
            dma((2,)),
            dma((back, heads)),
            dma((back, heads)),
            dma((own * group,)),
            dma((own * group,)),
            dma((n_tp - 1, group)),
            dma((n_tp - 1, group)),
            dma((n_tp - 1, tiles)),
            dma((n_tp - 1, tiles)),
        ],
        compiler_params=pltpu.CompilerParams(
            collective_id=0, has_side_effects=True, vmem_limit_bytes=44 << 20
        ),
    )(
        pltpu.with_memory_space_constraint(lengths, pltpu.HBM),
        pltpu.with_memory_space_constraint(flat(queries, group), pltpu.HBM),
        pltpu.with_memory_space_constraint(flat(pairs, 2), pltpu.HBM),
        out_proj.reshape(heads * width, model),
    )
    return result.reshape(1, rows, columns)


def solution(mesh):
    sizes = [mesh.shape[axis] for axis in ("segment", "ctx", "tp")]
    return jax.shard_map(
        functools.partial(local, *sizes),
        mesh=mesh,
        in_specs=(
            P("segment", "ctx", "tp", None),
            P("segment", "ctx", "tp", None),
            P("segment", "tp", None, None),
            P(),
        ),
        out_specs=P("segment", "ctx", "tp"),
        check_vma=False,
    )
```

time: 33 us -> 25.4 us (0.77)
  the two profiles are of different devices: /device:TPU:21 before, /device:TPU:29 now
where the time goes in v1:
time: 25.4 us; the launch traced here: 25.2 us
  Pallas kernels  24.4 us (96%)
  local copies, waits for them, and re-layouts  0.84 us (3%)
    pallas_call x1, Pallas kernels, local(): pl.pallas_call(functools.partial(kernel, sizes), out_shape=jax.ShapeDtype...  24.4 us
    unnamed x1, local copies, waits for them, and re-layouts  0.84 us

profile of v1, /device:TPU:29, one launch (start us, length us, event | category | flops | bytes accessed | tf_op | source)
XLA Modules:
  0.0 25.2 jit_solution(8448326897832478606)
XLA Ops:
  0.0 24.4 %shard_map.46 = bf16[128,2560]{1,0:T(8,128)(2,1)S(1)} custom-call(s32[4,4]{1,0:T(4,128)} %lengths_hbm.1, bf16[2560,128]{1,0:T(8,128)(2,1)} %bitcast.14, bf16[1024,128]{1,0:T(8,128)(2,1)} %bitcast.15, bf16[2560,5120]{1,0:T(8,128)(2,1)} %bitcast.13), custom_call_target="tpu_custom_call" | custom-call | tf_op jit(solution)/shard_map/pallas_call | solution.py:489
  24.4 0.8 %copy.6 = bf16[1,128,2560]{2,1,0:T(8,128)(2,1)} copy(bf16[1,128,2560]{2,1,0:T(8,128)(2,1)S(1)} %bitcast.12) | data formatting | bytes 1310720

commit v2 on v1

--- a/solution.py
+++ b/solution.py
@@ -75,6 +75,7 @@
     own = heads - shipped
     last = own - 1
     early = [h for h in range(heads) if h != last]
+    order = [h for h in early if h >= own] + [h for h in early if h < own]
     to_seg = lax.rem(seg + n_seg - 1, n_seg)
     from_seg = lax.rem(seg + 1, n_seg)
     relays = n_ctx == 4 and back == 2
@@ -176,6 +177,10 @@
         split_kv(own, ship_kv)
     q_copy.wait()
     q_wide[...] = q_raw[...].astype(jnp.float32)
+    for n in [early.index(h) for h in order]:
+        w_copy(n).start()
+    for g in range(group):
+        own_w_copy(g).start()
     if shipped:
         split_q(own, ship_q, 0)
 
@@ -223,10 +228,7 @@
             ship(n).start()
     for h in range(own):
         spread(h)
-    for n in range(len(early)):
-        w_copy(n).start()
     for g in range(group):
-        own_w_copy(g).start()
         for by in range(1, n_tp):
             peer_w_copy(by, g).start()
 
@@ -354,7 +356,6 @@
         ship(1).wait_recv()
         attend(own, 1, got_ref)
 
-    order = [h for h in early if h >= own] + [h for h in early if h < own]
 
     def share_copy(by, n):
         at = pl.ds(n * tile, tile)
@@ -426,12 +427,12 @@
                 total = total + share_ref[by - 1].astype(jnp.float32)
         out_ref[...] = total.astype(jnp.bfloat16)
 
+    for g in range(handed, min(group, 3)):
+        hand_on(g)
     for g in range(group):
-        if g >= handed:
-            hand_on(g)
-        if g > 0:
-            finish(g - 1)
-    finish(group - 1)
+        finish(g)
+        if g + 3 < group:
+            hand_on(g + 3)
 
     for unit in range(own * group):
         att_copy(unit).wait_send()

time: 25.4 us -> 24.2 us (0.953)
  the two profiles are of different devices: /device:TPU:29 before, /device:TPU:0 now
where the time goes in v2:
time: 24.2 us; the launch traced here: 24.1 us
  Pallas kernels  23.2 us (96%)
  local copies, waits for them, and re-layouts  0.84 us (3%)
    pallas_call x1, Pallas kernels, local(): pl.pallas_call(functools.partial(kernel, sizes), out_shape=jax.ShapeDtype...  23.2 us
    unnamed x1, local copies, waits for them, and re-layouts  0.84 us

profile of v2, /device:TPU:0, one launch (start us, length us, event | category | flops | bytes accessed | tf_op | source)
XLA Modules:
  0.0 24.1 jit_solution(15426476491852749462)
XLA Ops:
  0.0 23.2 %shard_map.46 = bf16[128,2560]{1,0:T(8,128)(2,1)S(1)} custom-call(s32[4,4]{1,0:T(4,128)} %lengths_hbm.1, bf16[2560,128]{1,0:T(8,128)(2,1)} %bitcast.14, bf16[1024,128]{1,0:T(8,128)(2,1)} %bitcast.15, bf16[2560,5120]{1,0:T(8,128)(2,1)} %bitcast.13), custom_call_target="tpu_custom_call" | custom-call | tf_op jit(solution)/shard_map/pallas_call | solution.py:490
  23.3 0.8 %copy.6 = bf16[1,128,2560]{2,1,0:T(8,128)(2,1)} copy(bf16[1,128,2560]{2,1,0:T(8,128)(2,1)S(1)} %bitcast.12) | data formatting | bytes 1310720

commit v3 on v2

--- a/solution.py
+++ b/solution.py
@@ -14,7 +14,7 @@
 
 
 def tile_of(columns):
-    for tile in (1280, 640, 512, 256, 128):
+    for tile in (512, 256, 128):
         if columns % tile == 0:
             return tile
     return columns
@@ -73,8 +73,9 @@
     tiles = columns // tile
     depth = (back + 1) * rows
     own = heads - shipped
-    last = own - 1
-    early = [h for h in range(heads) if h != last]
+    late = own - min(own, 2)
+    units = (own - late) * group
+    early = [h for h in range(heads) if not late <= h < own]
     order = [h for h in early if h >= own] + [h for h in early if h < own]
     to_seg = lax.rem(seg + n_seg - 1, n_seg)
     from_seg = lax.rem(seg + 1, n_seg)
@@ -136,7 +137,7 @@
     def own_w_copy(g):
         return pltpu.make_async_copy(
             w_hbm.at[
-                pl.ds(last * width + g * head_dim, head_dim),
+                pl.ds(late * width + g * head_dim, head_dim),
                 pl.ds(pl.multiple_of(tp * columns, columns), columns),
             ],
             last_w.at[g, pl.ds(0, head_dim)],
@@ -147,7 +148,7 @@
         peer = lax.rem(tp + by, n_tp)
         return pltpu.make_async_remote_copy(
             src_ref=w_hbm.at[
-                pl.ds(last * width + g * head_dim, head_dim),
+                pl.ds(late * width + g * head_dim, head_dim),
                 pl.ds(pl.multiple_of(peer * columns, columns), columns),
             ],
             dst_ref=last_w.at[g, pl.ds(by * head_dim, head_dim)],
@@ -179,7 +180,7 @@
     q_wide[...] = q_raw[...].astype(jnp.float32)
     for n in [early.index(h) for h in order]:
         w_copy(n).start()
-    for g in range(group):
+    for g in range(units):
         own_w_copy(g).start()
     if shipped:
         split_q(own, ship_q, 0)
@@ -228,7 +229,7 @@
             ship(n).start()
     for h in range(own):
         spread(h)
-    for g in range(group):
+    for g in range(units):
         for by in range(1, n_tp):
             peer_w_copy(by, g).start()
 
@@ -271,7 +272,7 @@
             device_id_type=MESH,
         )
 
-    def receive(h):
+    def pass_on(h):
         if relayed(h):
 
             @pl.when(ctx == 3)
@@ -279,6 +280,7 @@
                 kv_send(2, h).wait_recv()
                 relay(h).start()
 
+    def receive(h):
         for by in range(back, 0, -1):
             known = ctx >= by
             if relayed(h) and by == 2:
@@ -348,6 +350,8 @@
         attend(h, 0, sent_ref)
         for g in range(group):
             att_copy(h * group + g).start()
+        if h + 1 < heads:
+            pass_on(h + 1)
         if shipped and h == 0:
             ship(0).wait_recv()
             spread(own)
@@ -370,7 +374,7 @@
 
     def forward(by, g):
         return pltpu.make_async_remote_copy(
-            src_ref=got_ref.at[last * group + g],
+            src_ref=got_ref.at[late * group + g],
             dst_ref=peer_got.at[by - 1, g],
             send_sem=fwd_send.at[by - 1, g],
             recv_sem=fwd_recv.at[by - 1, g],
@@ -379,11 +383,10 @@
         )
 
     def hand_on(g):
-        att_copy(last * group + g).wait_recv()
+        att_copy(late * group + g).wait_recv()
         for by in range(1, n_tp):
             forward(by, g).start()
 
-    handed = 0
     for h in order:
         arrived(h)
         w_copy(early.index(h)).wait()
@@ -392,13 +395,11 @@
             continue
         for by in range(1, n_tp):
             peer = lax.rem(tp + by, n_tp)
-            for n in range(tiles):
-                part_ref[by - 1, :, pl.ds(n * tile, tile)] = total_of(
-                    early.index(h), peer * columns + n * tile, tile
-                ).astype(jnp.bfloat16)
-                share_copy(by, n).start()
-        handed = handed + 1
-        hand_on(0)
+            part_ref[by - 1] = total_of(
+                early.index(h), peer * columns, columns
+            ).astype(jnp.bfloat16)
+        for g in range(min(units, 2)):
+            hand_on(g)
         begin = pl.multiple_of(tp * columns, columns)
         acc_ref[:, pl.ds(begin, columns)] = total_of(
             early.index(h), begin, columns
@@ -410,29 +411,35 @@
             peer_w_copy(by, g).wait_recv()
             forward(by, g).wait_recv()
         mixed = jnp.concatenate(
-            [got_ref[last * group + g]] + [peer_got[by - 1, g] for by in range(1, n_tp)],
+            [got_ref[late * group + g]] + [peer_got[by - 1, g] for by in range(1, n_tp)],
             axis=1,
         )
         into = pl.ds(pl.multiple_of(tp * columns, columns), columns)
         total = jnp.dot(mixed, last_w[g], preferred_element_type=jnp.float32)
         if order or g > 0:
             total = total + acc_ref[:, into]
-        if g < group - 1:
-            acc_ref[:, into] = total
-            return
-        if order:
+        if order and g == sum_at:
             for by in range(1, n_tp):
                 for n in range(tiles):
                     share_copy(by, n).wait_recv()
                 total = total + share_ref[by - 1].astype(jnp.float32)
+        if g < units - 1:
+            acc_ref[:, into] = total
+            return
         out_ref[...] = total.astype(jnp.bfloat16)
 
-    for g in range(handed, min(group, 3)):
-        hand_on(g)
-    for g in range(group):
+    sum_at = max(0, units - 3)
+    handed = min(units, 2) if order else 0
+    for g in range(units):
+        for ahead in range(handed, min(units, g + 4)):
+            hand_on(ahead)
+        handed = max(handed, min(units, g + 4))
+        if order:
+            for n in range(tiles):
+                if min(n, sum_at) == g:
+                    for by in range(1, n_tp):
+                        share_copy(by, n).start()
         finish(g)
-        if g + 3 < group:
-            hand_on(g + 3)
 
     for unit in range(own * group):
         att_copy(unit).wait_send()
@@ -453,7 +460,7 @@
         for n in range(2):
             ship(n).wait_send()
     for by in range(1, n_tp):
-        for g in range(group):
+        for g in range(units):
             peer_w_copy(by, g).wait_send()
             forward(by, g).wait_send()
         if order:
@@ -475,6 +482,8 @@
     tiles = columns // tile_of(columns)
     shipped = 1 if heads > 1 else 0
     own = heads - shipped
+    units = min(own, 2) * group
+    kept = max(1, heads - min(own, 2))
     sizes = (n_seg, n_ctx, n_tp, rows, heads, head_dim, group, back, shipped)
     bf16, f32 = jnp.bfloat16, jnp.float32
     dma = pltpu.SemaphoreType.DMA
@@ -502,35 +511,35 @@
             pltpu.VMEM((heads, rows, 2 * head_dim), bf16),
             pltpu.VMEM((group, rows, head_dim), bf16),
             pltpu.VMEM((rows, 2 * head_dim), bf16),
-            pltpu.VMEM((max(1, heads - 1) * width, model), bf16),
-            pltpu.VMEM((group, n_tp * head_dim, columns), bf16),
+            pltpu.VMEM((kept * width, model), bf16),
+            pltpu.VMEM((units, n_tp * head_dim, columns), bf16),
             pltpu.VMEM((heads, back, rows, 2 * head_dim), bf16),
             pltpu.VMEM((1 + shipped, rows, (back + 1) * rows), f32),
             pltpu.VMEM((own * group, rows, head_dim), bf16),
             pltpu.VMEM((heads * group, rows, head_dim), bf16),
-            pltpu.VMEM((n_tp - 1, group, rows, head_dim), bf16),
+            pltpu.VMEM((n_tp - 1, units, rows, head_dim), bf16),
             pltpu.VMEM((rows, model), f32),
             pltpu.VMEM((n_tp - 1, rows, columns), bf16),
             pltpu.VMEM((n_tp - 1, rows, columns), bf16),
             dma,
             dma((2,)),
-            dma((max(1, heads - 1),)),
-            dma((group,)),
-            dma((n_tp - 1, group)),
-            dma((n_tp - 1, group)),
+            dma((kept,)),
+            dma((units,)),
+            dma((n_tp - 1, units)),
+            dma((n_tp - 1, units)),
             dma((2,)),
             dma((2,)),
             dma((back, heads)),
             dma((back, heads)),
             dma((own * group,)),
             dma((own * group,)),
-            dma((n_tp - 1, group)),
-            dma((n_tp - 1, group)),
+            dma((n_tp - 1, units)),
+            dma((n_tp - 1, units)),
             dma((n_tp - 1, tiles)),
             dma((n_tp - 1, tiles)),
         ],
         compiler_params=pltpu.CompilerParams(
-            collective_id=0, has_side_effects=True, vmem_limit_bytes=44 << 20
+            collective_id=0, has_side_effects=True, vmem_limit_bytes=48 << 20
         ),
     )(
         pltpu.with_memory_space_constraint(lengths, pltpu.HBM),

time: 24.2 us -> 23.8 us (0.983)
  Pallas kernels: 23.2 us -> 22.9 us
    pallas_call x1, Pallas kernels: 23.2 us -> 22.9 us  [local(): pl.pallas_call(functools.partial(kernel, sizes), out_shape=jax.ShapeDtype...]
where the time goes in v3:
time: 23.8 us; the launch traced here: 23.7 us
  Pallas kernels  22.9 us (96%)
  local copies, waits for them, and re-layouts  0.84 us (4%)
    pallas_call x1, Pallas kernels, local(): pl.pallas_call(functools.partial(kernel, sizes), out_shape=jax.ShapeDtype...  22.9 us
    unnamed x1, local copies, waits for them, and re-layouts  0.84 us

profile of v3, /device:TPU:0, one launch (start us, length us, event | category | flops | bytes accessed | tf_op | source)
XLA Modules:
  0.0 23.7 jit_solution(4871158274915713855)
XLA Ops:
  0.0 22.9 %shard_map.46 = bf16[128,2560]{1,0:T(8,128)(2,1)S(1)} custom-call(s32[4,4]{1,0:T(4,128)} %lengths_hbm.1, bf16[2560,128]{1,0:T(8,128)(2,1)} %bitcast.14, bf16[1024,128]{1,0:T(8,128)(2,1)} %bitcast.15, bf16[2560,5120]{1,0:T(8,128)(2,1)} %bitcast.13), custom_call_target="tpu_custom_call" | custom-call | tf_op jit(solution)/shard_map/pallas_call | solution.py:499
  22.9 0.8 %copy.6 = bf16[1,128,2560]{2,1,0:T(8,128)(2,1)} copy(bf16[1,128,2560]{2,1,0:T(8,128)(2,1)S(1)} %bitcast.12) | data formatting | bytes 1310720
